TPU v7x, 256 devices: a whole 4x4x8 slice. The times are simulated.
256 devices in a mesh: grid: 64 (over y, z, core), rep: 4 (over x).
Axes of the slice: x: 4, y: 4, z: 8, core: 2. Of those that a mesh axis runs over, the one named last changes fastest.
Arguments:
- integrals: bfloat16 [131072, 512], P(('grid', 'rep')), may hold values from -6 to 6
- green_occ: bfloat16 [512, 16384], P(None, 'grid'), may hold values from -0.25 to 0.25
- tile_panels: int32 [1024, 16], P(('grid', 'rep')), may hold values from 0 to 63, all different within a row; in each aligned block of 4 rows (0 to 3, 4 to 7, ...) at most 2 rows name the same one
- virtual_blocks: bfloat16 [64, 16, 256, 256], P('grid', 'rep'), may hold values from -0.0234375 to 0.0234375
Outputs:
- response_blocks: float32 [64, 128, 256], P('grid', 'rep')
Inputs may be any that keep to these rules, and one draw needn't show every extreme that they name: `tile_panels`: each row lists 16 different panels. In each aligned block of 4 rows (the tiles of one device) no panel is listed by more than 2 rows, and some panel is listed by exactly 2 rows.
All inputs are finite; a program needn't handle non-finite values.
Results may differ from a plain program's by a relative error of at most 0.0029.
Values may be sent and summed in bfloat16 or wider, within the bound.
A program may use at most 128 MiB of HBM per device.

v0:
```python
import jax
import jax.numpy as jnp
from jax import lax
from jax.sharding import PartitionSpec as P

CAP = 2


def shards(integrals, green_occ, tile_panels, virtual_blocks):
    grid_count = lax.axis_size("grid")
    tile_count = tile_panels.shape[0]
    tile_rows = integrals.shape[0] // tile_count
    panel_width = green_occ.shape[1]
    owners = jnp.arange(grid_count, dtype=jnp.int32)
    hit_count = jnp.sum(
        (tile_panels[:, :, None] == owners[None, None, :]).astype(jnp.int32), axis=1
    )
    before = jnp.cumsum(hit_count, axis=0) - hit_count
    slot_ids = jnp.arange(CAP, dtype=jnp.int32)
    placement = (hit_count[:, :, None] == 1) & (before[:, :, None] == slot_ids[None, None, :])
    place_weights = placement.astype(jnp.bfloat16)
    tile_ids = jnp.arange(tile_count, dtype=jnp.int32)
    labels = jnp.sum(placement.astype(jnp.int32) * tile_ids[:, None, None], axis=0)
    contracted = jnp.dot(
        integrals,
        lax.all_gather(green_occ, "grid", axis=1, tiled=True),
        preferred_element_type=jnp.float32,
    ).astype(jnp.bfloat16)
    tile_blocks = contracted.reshape(tile_count, tile_rows, grid_count, panel_width)
    outgoing = jnp.einsum(
        "ldc,ltdw->dctw", place_weights, tile_blocks, preferred_element_type=jnp.float32
    ).astype(jnp.bfloat16)
    arrived, got_labels = (
        lax.all_to_all(outgoing, "grid", split_axis=0, concat_axis=0, tiled=True),
        lax.all_to_all(labels, "grid", split_axis=0, concat_axis=0, tiled=True),
    )
    slot_owner = (got_labels[:, :, None] == tile_ids[None, None, :]).astype(jnp.bfloat16)
    summed = jnp.einsum("gcl,gctw->ltw", slot_owner, arrived, preferred_element_type=jnp.float32)
    owner_part = jnp.einsum(
        "ltw,lwc->tc",
        summed,
        virtual_blocks[0].astype(jnp.float32),
        precision=lax.Precision.HIGHEST,
    )
    return lax.psum_scatter(owner_part[None], "rep", scatter_dimension=1, tiled=True)


def solution(mesh):
    in_specs = (
        P(("grid", "rep"), None),
        P(None, "grid"),
        P(("grid", "rep"), None),
        P("grid", "rep", None, None),
    )
    out_specs = P("grid", "rep", None)
    return jax.shard_map(shards, mesh=mesh, in_specs=in_specs, out_specs=out_specs, check_vma=False)
```

profile of v0, /device:TPU:8, one launch (start us, length us, event | category | flops | bytes accessed | tf_op | source)
XLA Modules:
  0.0 416.4 jit_solution(14238982077939714297)
XLA Ops:
  6.5 0.0 copy-start
  6.5 0.0 all-gather.2.cloned.1.call-start
  6.5 0.7 all-gather.2.cloned.1.call-update
  7.3 0.8 convert_reduce_fusion
  8.1 0.7 copy.9
  8.8 12.1 %all-to-all-start = ((s32[64,1,2]{2,1,0:T(1,128)}), s32[64,1,2]{2,1,0:T(1,128)S(1)}, u32[]{:S(2)}, u32[]{:S(2)}) async-start(s32[64,1,2]{2,1,0:T(1,128)} %copy.9), calls=%async_computation | async-start | bytes 65536 | tf_op jit(solution)/shard_map/all_to_all | solution.py:35
  21.0 0.1 copy.15
  21.1 96.2 %all-gather.2.cloned.1.call-done = bf16[512,16384]{1,0:T(8,128)(2,1)} async-done(((bf16[512,256]{1,0:T(8,128)(2,1)}), bf16[512,16384]{1,0:T(8,128)(2,1)}) %all-gather.2.cloned.1.call-update) | async-done | bytes 16777232 | tf_op jit(solution)/shard_map/all_gather | solution.py:26
  117.3 0.0 copy-done
  117.3 18.0 %convolution_convert_fusion = bf16[512,16384]{1,0:T(8,128)(2,1)} fusion(bf16[512,512]{1,0:T(8,128)(2,1)S(1)} %copy-done, bf16[512,16384]{1,0:T(8,128)(2,1)} %all-gather.2.cloned.1.call-done), kind=kOutput, calls=%fused_computation | convolution fusion | flops 8598323200 | bytes 34078720 | tf_op jit(solution)/shard_map/dot_general | solution.py:24
  135.4 10.3 %copy.19 = bf16[64,8,64,256]{3,2,1,0:T(8,128)(2,1)S(1)} copy(bf16[64,8,64,256]{3,1,2,0:T(8,128)(2,1)} %bitcast.23) | data formatting | bytes 33554432
  145.6 0.0 copy-start.1
  145.6 35.7 %fusion.2 = bf16[64,2,128,256]{3,1,2,0:T(2,128)(2,1)} fusion(pred[4,64,2,1]{0,2,3,1:T(4,128)(4,1)S(1)} %copy.15, bf16[4,128,64,256]{3,2,1,0:T(8,128)(2,1)S(1)} %bitcast.22), kind=kOutput, calls=%fused_computation.3 | convolution fusion | flops 37748736 | bytes 25166336 | tf_op jit(solution)/shard_map/ldc,ltdw->dctw/dot_general | solution.py:30
  181.4 0.0 copy-start.2
  181.4 0.0 all-to-all-done
  181.4 9.3 %all-to-all-start.1 = ((bf16[64,2,128,256]{3,1,2,0:T(2,128)(2,1)}), bf16[64,2,128,256]{3,1,2,0:T(2,128)(2,1)}, u32[]{:S(2)}, u32[]{:S(2)}) async-start(bf16[64,2,128,256]{3,1,2,0:T(2,128)(2,1)} %fusion.2), calls=%async_computation.1 | async-start | bytes 16777216 | tf_op jit(solution)/shard_map/all_to_all | solution.py:34
  190.6 0.0 reduce-scatter.2.cloned.1.call-start
  190.7 0.1 copy.10
  190.8 184.1 %all-to-all-done.1 = bf16[64,2,128,256]{3,1,2,0:T(2,128)(2,1)} async-done(((bf16[64,2,128,256]{3,1,2,0:T(2,128)(2,1)}), bf16[64,2,128,256]{3,1,2,0:T(2,128)(2,1)}, u32[]{:S(2)}, u32[]{:S(2)}) %all-to-all-start.1) | async-done | bytes 8388640 | tf_op jit(solution)/shard_map/all_to_all | solution.py:34
  374.9 12.2 %fusion.7 = f32[4,128,256]{2,0,1:T(4,128)S(1)} fusion(bf16[64,2,128,256]{3,1,2,0:T(2,128)(2,1)} %all-to-all-done.1, s32[64,2]{0,1:T(2,128)S(1)} %bitcast.24), kind=kOutput, calls=%fused_computation.6 | convolution fusion | flops 33554944 | bytes 8913408 | tf_op jit(solution)/shard_map/gcl,gctw->ltw/dot_general | solution.py:38
  387.1 0.0 copy-done.2
  387.1 1.1 convolution_bitcast_fusion
  388.2 0.0 reduce-scatter.2.cloned.1.call-update
  388.2 21.4 %reduce-scatter.2.cloned.1.call-done = f32[1,32,256]{2,1,0:T(8,128)} async-done(((f32[1,128,256]{2,1,0:T(8,128)}), f32[1,32,256]{2,1,0:T(8,128)}) %reduce-scatter.2.cloned.1.call-update) | async-done | bytes 32784 | tf_op jit(solution)/shard_map/reduce_scatter | solution.py:45
  409.6 0.0 copy-done.1
  (5 shorter events, 0.1 us)
Async XLA Ops:
  6.5 110.8 %copy-start = (bf16[512,512]{1,0:T(8,128)(2,1)S(1)}, bf16[512,512]{1,0:T(8,128)(2,1)}, u32[]{:S(2)}) copy-start(bf16[512,512]{1,0:T(8,128)(2,1)} %param.4) | copy-start | bytes 1572868
  6.5 110.8 %all-gather.2.cloned.1.call-start = ((), (), s32[]{:S(2)}) async-start(), calls=%async_computation.3 | async-start | bytes 17039360 | tf_op jit(solution)/shard_map/all_gather | solution.py:26
  8.8 172.6 %all-to-all-start = ((s32[64,1,2]{2,1,0:T(1,128)}), s32[64,1,2]{2,1,0:T(1,128)S(1)}, u32[]{:S(2)}, u32[]{:S(2)}) async-start(s32[64,1,2]{2,1,0:T(1,128)} %copy.9), calls=%async_computation | async-start | bytes 65536 | tf_op jit(solution)/shard_map/all_to_all | solution.py:35
  145.6 264.0 %copy-start.1 = (bf16[512,512]{1,0:T(8,128)(2,1)S(1)}, bf16[512,512]{1,0:T(8,128)(2,1)}, u32[]{:S(2)}) copy-start(bf16[512,512]{1,0:T(8,128)(2,1)} %param.4) | copy-start | bytes 1572868
  181.4 205.7 %copy-start.2 = (bf16[1,4,256,256]{3,2,1,0:T(8,128)(2,1)S(1)}, bf16[1,4,256,256]{3,2,1,0:T(8,128)(2,1)}, u32[]{:S(2)}) copy-start(bf16[1,4,256,256]{3,2,1,0:T(8,128)(2,1)} %param.7) | copy-start | bytes 1572868
  181.4 193.5 %all-to-all-start.1 = ((bf16[64,2,128,256]{3,1,2,0:T(2,128)(2,1)}), bf16[64,2,128,256]{3,1,2,0:T(2,128)(2,1)}, u32[]{:S(2)}, u32[]{:S(2)}) async-start(bf16[64,2,128,256]{3,1,2,0:T(2,128)(2,1)} %fusion.2), calls=%async_computation.1 | async-start | bytes 16777216 | tf_op jit(solution)/shard_map/all_to_all | solution.py:34
  190.6 218.9 %reduce-scatter.2.cloned.1.call-start = ((), (), s32[]{:S(2)}) async-start(), calls=%async_computation.4 | async-start | bytes 163840 | tf_op jit(solution)/shard_map/reduce_scatter | solution.py:45
Sparse Core Ops, SparseCore 0:
  9.9 107.3 all-gather.1
  388.3 21.1 reduce-scatter.1
where the time goes:
time: 417 us; the launch traced here: 416 us
  waiting for transfers between devices  302 us (72%)
  matrix products  67.1 us (16%)
  starting transfers between devices  21.4 us (5%)
  between operations  13.5 us (3%)
  local copies, waits for them, and re-layouts  11.2 us (3%)
    all_to_all x1, waiting for transfers between devices, shards(): lax.all_to_all(outgoing, 'grid', split_axis=0, concat_axis=0, tiled=True)  184 us
    all_gather x1, waiting for transfers between devices, shards(): lax.all_gather(green_occ, 'grid', axis=1, tiled=True)  96.2 us
    dot_general x1, matrix products, shards(): jnp.einsum('ldc,ltdw->dctw', place_weights, tile_blocks, preferred_elemen...  35.7 us
    reduce_scatter x1, waiting for transfers between devices, shards(): lax.psum_scatter(owner_part[None], 'rep', scatter_dimension=1, tiled=True)  21.4 us
    dot_general x1, matrix products, shards(): jnp.dot(integrals, lax.all_gather(green_occ, 'grid', axis=1, tiled=True),...  18 us
    dot_general x1, matrix products, shards(): jnp.einsum('gcl,gctw->ltw', slot_owner, arrived, preferred_element_type=j...  12.2 us
    all_to_all x1, starting transfers between devices, shards(): lax.all_to_all(labels, 'grid', split_axis=0, concat_axis=0, tiled=True)  12.1 us
    unnamed x7, local copies, waits for them, and re-layouts  10.3 us
  transfers between devices with their start and end apart: 4, of which 3 were waited for; matrix products, arithmetic and copies ran while one was open for 16% of the time, Pallas kernels for 0%

commit v1 on v0

--- a/solution.py
+++ b/solution.py
@@ -23,7 +23,9 @@
     labels = jnp.sum(placement.astype(jnp.int32) * tile_ids[:, None, None], axis=0)
     contracted = jnp.dot(
         integrals,
-        lax.all_gather(green_occ, "grid", axis=1, tiled=True),
+        jnp.concatenate(
+            lax.all_to_all(jnp.stack([green_occ] * lax.axis_size("grid")), "grid", 0, 0), axis=1
+        ),
         preferred_element_type=jnp.float32,
     ).astype(jnp.bfloat16)
     tile_blocks = contracted.reshape(tile_count, tile_rows, grid_count, panel_width)

time: 417 us -> 691 us (1.66)
  waiting for transfers between devices: 302 us -> 569 us
  starting transfers between devices: 21.4 us -> 29.3 us
  matrix products: 67.1 us -> 59.3 us
    all_to_all x0 -> x1, waiting for transfers between devices: none -> 363 us  [shards(): lax.all_to_all(jnp.stack([green_occ] * lax.axis_size('grid')), 'grid', 0, 0)]
    all_gather x1 -> x0, waiting for transfers between devices: 96.2 us -> none  [shards(): lax.all_gather(green_occ, 'grid', axis=1, tiled=True)]
    all_to_all x0 -> x1, starting transfers between devices: none -> 12.4 us  [shards(): lax.all_to_all(jnp.stack([green_occ] * lax.axis_size('grid')), 'grid', 0, 0)]
    dot_general x1, matrix products: 35.7 us -> 27.2 us  [shards(): jnp.einsum('ldc,ltdw->dctw', place_weights, tile_blocks, preferred_elemen...]
  transfers between devices with their start and end apart: 4 -> 4, of which waited for: 3 -> 3; matrix products, arithmetic and copies ran while one was open for 16% -> 8% of each run, Pallas kernels for 0% -> 0%
where the time goes in v1:
time: 691 us; the launch traced here: 690 us
  waiting for transfers between devices  569 us (82%)
  matrix products  59.3 us (9%)
  starting transfers between devices  29.3 us (4%)
  local copies, waits for them, and re-layouts  17.7 us (3%)
  between operations  13.5 us (2%)
    all_to_all x1, waiting for transfers between devices, shards(): lax.all_to_all(jnp.stack([green_occ] * lax.axis_size('grid')), 'grid', 0, 0)  363 us
    all_to_all x1, waiting for transfers between devices, shards(): lax.all_to_all(outgoing, 'grid', split_axis=0, concat_axis=0, tiled=True)  184 us
    dot_general x1, matrix products, shards(): jnp.einsum('ldc,ltdw->dctw', place_weights, tile_blocks, preferred_elemen...  27.2 us
    reduce_scatter x1, waiting for transfers between devices, shards(): lax.psum_scatter(owner_part[None], 'rep', scatter_dimension=1, tiled=True)  21.4 us
    dot_general x1, matrix products, shards(): jnp.dot(integrals, jnp.concatenate(lax.all_to_all(jnp.stack([green_occ] *...  18.9 us
  transfers between devices with their start and end apart: 4, of which 3 were waited for; matrix products, arithmetic and copies ran while one was open for 8% of the time, Pallas kernels for 0%

profile of v1, /device:TPU:8, one launch (start us, length us, event | category | flops | bytes accessed | tf_op | source)
XLA Modules:
  0.0 690.2 jit_solution(9280723597258465777)
XLA Ops:
  6.5 0.0 copy-start
  6.5 1.1 copy.26
  7.7 6.0 stack.2
  13.7 0.0 copy-start.3
  13.7 12.4 %all-to-all-start.1 = ((bf16[64,512,256]{1,2,0:T(8,128)(2,1)}), bf16[64,512,256]{1,2,0:T(8,128)(2,1)}, u32[]{:S(2)}, u32[]{:S(2)}) async-start(bf16[64,512,256]{1,2,0:T(8,128)(2,1)} %stack.2), calls=%async_computation.1 | async-start | bytes 33554432 | tf_op jit(solution)/shard_map/all_to_all | solution.py:27
  26.1 0.0 copy-done.3
  26.1 0.1 convert_reduce_fusion
  26.2 0.1 copy.21
  26.4 0.1 copy.22
  26.5 1.8 select_reduce_fusion
  28.3 363.0 %all-to-all-done.1 = bf16[64,512,256]{1,2,0:T(8,128)(2,1)} async-done(((bf16[64,512,256]{1,2,0:T(8,128)(2,1)}), bf16[64,512,256]{1,2,0:T(8,128)(2,1)}, u32[]{:S(2)}, u32[]{:S(2)}) %all-to-all-start.1) | async-done | bytes 16777248 | tf_op jit(solution)/shard_map/all_to_all | solution.py:27
  391.2 6.2 all-to-all-start
  397.4 0.0 copy-done
  397.4 18.9 %convolution_convert_fusion = bf16[512,16384]{1,0:T(8,128)(2,1)} fusion(bf16[512,512]{1,0:T(8,128)(2,1)S(1)} %copy-done, bf16[512,16384]{0,1:T(8,128)(2,1)} %bitcast.6), kind=kOutput, calls=%fused_computation | convolution fusion | flops 8598323200 | bytes 34078720 | tf_op jit(solution)/shard_map/dot_general | solution.py:24
  416.3 10.3 %copy.34 = bf16[64,8,64,256]{3,2,1,0:T(8,128)(2,1)S(1)} copy(bf16[64,8,64,256]{3,1,2,0:T(8,128)(2,1)} %bitcast.30) | data formatting | bytes 33554432
  426.6 0.0 copy-start.1
  426.6 27.2 %fusion.2 = bf16[64,2,128,256]{3,1,2,0:T(2,128)(2,1)} fusion(bf16[4,128,64,256]{3,2,1,0:T(8,128)(2,1)S(1)} %bitcast.29, pred[4,64]{0,1:T(8,128)(4,1)S(1)} %copy.21, s32[4,64]{0,1:T(8,128)S(1)} %copy.22), kind=kOutput, calls=%fused_computation.3 | convolution fusion | flops 37749760 | bytes 25167104 | tf_op jit(solution)/shard_map/ldc,ltdw->dctw/dot_general | solution.py:32
  453.7 0.0 copy-start.2
  453.7 0.0 all-to-all-done
  453.7 10.6 %all-to-all-start.2 = ((bf16[64,2,128,256]{3,1,2,0:T(2,128)(2,1)}), bf16[64,2,128,256]{3,1,2,0:T(2,128)(2,1)}, u32[]{:S(2)}, u32[]{:S(2)}) async-start(bf16[64,2,128,256]{3,1,2,0:T(2,128)(2,1)} %fusion.2), calls=%async_computation.2 | async-start | bytes 16777216 | tf_op jit(solution)/shard_map/all_to_all | solution.py:36
  464.4 0.0 reduce-scatter.2.cloned.1.call-start
  464.4 0.1 copy.25
  464.5 184.1 %all-to-all-done.2 = bf16[64,2,128,256]{3,1,2,0:T(2,128)(2,1)} async-done(((bf16[64,2,128,256]{3,1,2,0:T(2,128)(2,1)}), bf16[64,2,128,256]{3,1,2,0:T(2,128)(2,1)}, u32[]{:S(2)}, u32[]{:S(2)}) %all-to-all-start.2) | async-done | bytes 8388640 | tf_op jit(solution)/shard_map/all_to_all | solution.py:36
  648.6 12.2 %fusion.7 = f32[4,128,256]{2,0,1:T(4,128)S(1)} fusion(bf16[64,2,128,256]{3,1,2,0:T(2,128)(2,1)} %all-to-all-done.2, s32[64,2]{0,1:T(2,128)S(1)} %bitcast.31), kind=kOutput, calls=%fused_computation.6 | convolution fusion | flops 33554944 | bytes 8913408 | tf_op jit(solution)/shard_map/gcl,gctw->ltw/dot_general | solution.py:40
  660.9 0.0 copy-done.2
  660.9 1.1 convolution_bitcast_fusion
  661.9 0.0 reduce-scatter.2.cloned.1.call-update
  662.0 21.4 %reduce-scatter.2.cloned.1.call-done = f32[1,32,256]{2,1,0:T(8,128)} async-done(((f32[1,128,256]{2,1,0:T(8,128)}), f32[1,32,256]{2,1,0:T(8,128)}) %reduce-scatter.2.cloned.1.call-update) | async-done | bytes 32784 | tf_op jit(solution)/shard_map/reduce_scatter | solution.py:47
  683.4 0.0 copy-done.1
  (3 shorter events, 0.1 us)
Async XLA Ops:
  6.5 390.9 %copy-start = (bf16[512,512]{1,0:T(8,128)(2,1)S(1)}, bf16[512,512]{1,0:T(8,128)(2,1)}, u32[]{:S(2)}) copy-start(bf16[512,512]{1,0:T(8,128)(2,1)} %param.4) | copy-start | bytes 1572868
  13.7 12.4 %copy-start.3 = (s32[4,16]{1,0:T(4,128)S(1)}, s32[4,16]{1,0:T(4,128)}, u32[]{:S(2)}) copy-start(s32[4,16]{1,0:T(4,128)} %param.6) | copy-start | bytes 772
  13.7 377.6 %all-to-all-start.1 = ((bf16[64,512,256]{1,2,0:T(8,128)(2,1)}), bf16[64,512,256]{1,2,0:T(8,128)(2,1)}, u32[]{:S(2)}, u32[]{:S(2)}) async-start(bf16[64,512,256]{1,2,0:T(8,128)(2,1)} %stack.2), calls=%async_computation.1 | async-start | bytes 33554432 | tf_op jit(solution)/shard_map/all_to_all | solution.py:27
  391.2 62.5 %all-to-all-start = ((s32[64,1,2]{2,1,0:T(1,128)}), s32[64,1,2]{2,1,0:T(1,128)S(1)}, u32[]{:S(2)}, u32[]{:S(2)}) async-start(s32[64,1,2]{2,1,0:T(1,128)} %bitcast.12), calls=%async_computation | async-start | bytes 65536 | tf_op jit(solution)/shard_map/all_to_all | solution.py:37
  426.6 256.8 %copy-start.1 = (bf16[512,512]{1,0:T(8,128)(2,1)S(1)}, bf16[512,512]{1,0:T(8,128)(2,1)}, u32[]{:S(2)}) copy-start(bf16[512,512]{1,0:T(8,128)(2,1)} %param.4) | copy-start | bytes 1572868
  453.7 207.1 %copy-start.2 = (bf16[1,4,256,256]{3,2,1,0:T(8,128)(2,1)S(1)}, bf16[1,4,256,256]{3,2,1,0:T(8,128)(2,1)}, u32[]{:S(2)}) copy-start(bf16[1,4,256,256]{3,2,1,0:T(8,128)(2,1)} %param.7) | copy-start | bytes 1572868
  453.7 194.9 %all-to-all-start.2 = ((bf16[64,2,128,256]{3,1,2,0:T(2,128)(2,1)}), bf16[64,2,128,256]{3,1,2,0:T(2,128)(2,1)}, u32[]{:S(2)}, u32[]{:S(2)}) async-start(bf16[64,2,128,256]{3,1,2,0:T(2,128)(2,1)} %fusion.2), calls=%async_computation.2 | async-start | bytes 16777216 | tf_op jit(solution)/shard_map/all_to_all | solution.py:36
  464.4 219.0 %reduce-scatter.2.cloned.1.call-start = ((), (), s32[]{:S(2)}) async-start(), calls=%async_computation.4 | async-start | bytes 163840 | tf_op jit(solution)/shard_map/reduce_scatter | solution.py:47
Sparse Core Ops, SparseCore 0:
  662.1 21.2 reduce-scatter.1
